TPU v7x, 128 devices: a whole 4x4x4 slice. The times are simulated.
128 devices in a mesh: gx: 16 (over x, y), gy: 8 (over z, core).
Axes of the slice: x: 4, y: 4, z: 4, core: 2. Of those that a mesh axis runs over, the one named last changes fastest.
Arguments:
- fine: bfloat16 [4096, 8, 256, 128], P(('gx', 'gy')), may hold values from -1500 to 1500
- patch_count: int32 [128], P(('gx', 'gy')), may hold values from 0 to 32, as said below
- block_place: int32 [128, 16], P(('gx', 'gy')), may hold values from 0 to 15, each once within a row
Outputs:
- factor: float32 [128, 128], replicated
- modes: bfloat16 [524288, 128], P(('gx', 'gy'))
Inputs may be any that keep to these rules, and one draw needn't show every extreme that they name: `patch_count`: devices 2k and 2k + 1 in the numbering d = (index along gx) * 8 + (index along gy) hold 32 patches together; in every draw some even device holds 32 and some odd device holds 32.
All inputs are finite; a program needn't handle non-finite values.
Results may differ from a plain program's by a relative error of at most 0.004.
The roundings to bfloat16 on the way count: a program that leaves them out, or rounds other values in their place, can miss the bound.
Values may be sent and summed in bfloat16 or wider, within the bound.
No kernel may reach another device: no remote copies, remote signals or barrier semaphores. Data moves between devices by JAX's collectives and lax.ppermute only.
A program may use at most 64 MiB of HBM per device.

v0:
```python
import functools

import jax
import jax.numpy as jnp
from jax import lax
from jax.sharding import Mesh
from jax.sharding import PartitionSpec as P

GY = ("gy_0", "gy_1")
GX = ("gx_0", "gx_1")
GX_GY = ("gx_0", "gx_1", "gy_0", "gy_1")


def swapped(value, axis, apart):
    mask = 2**apart
    pairs = [(source, source ^ mask) for source in range(lax.axis_size(axis))]
    return lax.ppermute(value, axis, pairs)


def by_axis(x, axes):
    return functools.reduce(lax.psum, axes, x)


def restrict_block(fine_block):
    return (jnp.sum(fine_block, axis=1, dtype=jnp.float32) * 0.125).astype(jnp.bfloat16)


def pick_rows(own_rows, moved_rows, wanted, slot_total):
    from_own = jnp.take(own_rows, jnp.clip(wanted, 0, slot_total - 1), axis=0)
    from_moved = jnp.take(
        moved_rows, jnp.clip(wanted - slot_total, 0, moved_rows.shape[0] - 1), axis=0
    )
    is_own = (wanted < slot_total).reshape((-1,) + (1,) * (own_rows.ndim - 1))
    return jnp.where(is_own, from_own, from_moved)


def lower_factor(gram):
    width = gram.shape[0]
    index_col = jnp.arange(width, dtype=jnp.int32)

    def column_step(column, lower):
        partial_col = gram[:, column] - jnp.dot(
            lower, lower[column], precision=lax.Precision.HIGHEST
        )
        pivot = jnp.sqrt(partial_col[column])
        values = jnp.where(
            index_col > column, partial_col / pivot, jnp.where(index_col == column, pivot, 0.0)
        )
        marker = (index_col == column).astype(jnp.float32)
        return lower + values[:, None] * marker[None, :]

    return lax.fori_loop(0, width, column_step, jnp.zeros((width, width), jnp.float32))


def lower_inverse(lower):
    width = lower.shape[0]
    index_col = jnp.arange(width, dtype=jnp.int32)
    identity = jnp.eye(width, dtype=jnp.float32)

    def row_step(row, inverse):
        known = jnp.where(index_col < row, lower[row], 0.0)
        values = (identity[row] - jnp.dot(known, inverse, precision=lax.Precision.HIGHEST)) / lower[
            row, row
        ]
        marker = (index_col == row).astype(jnp.float32)
        return inverse + marker[:, None] * values[None, :]

    return lax.fori_loop(0, width, row_step, jnp.zeros((width, width), jnp.float32))


def upper_factor(gram):
    return lower_factor(gram).T


def shards(fine, patch_count, block_place):
    slot_total = fine.shape[0]
    blocks = slot_total // 2
    patch_cells = fine.shape[2]
    width = fine.shape[3]
    parity = lax.axis_index(GY) % 2
    held_count = patch_count[0]
    excess = jnp.where(parity == 0, held_count - blocks, blocks - held_count)
    local_ids = jnp.arange(blocks, dtype=jnp.int32)
    even_index = jnp.where(
        local_ids < blocks + excess, local_ids, slot_total + local_ids - blocks - excess
    )
    odd_index = jnp.where(local_ids < excess, slot_total + local_ids, local_ids - excess)
    chosen_index = jnp.where(parity == 0, even_index, odd_index)
    ordering = jnp.take(chosen_index, block_place[0], axis=0)
    send_first = (1 - parity) * blocks
    averaged = restrict_block(fine)
    outgoing = lax.dynamic_slice_in_dim(averaged, send_first, blocks, 0)
    incoming = swapped(outgoing, GY, 0)
    coarse = pick_rows(averaged, incoming, ordering, slot_total)
    coarse_rows = coarse.reshape(blocks * patch_cells, width)
    row_total = coarse_rows.shape[0] * lax.axis_size(GX) * lax.axis_size(GY)
    local_gram = (
        lax.dot_general(
            coarse_rows, coarse_rows, (((0,), (0,)), ((), ())), preferred_element_type=jnp.float32
        )
        / row_total
    )
    gram = by_axis(local_gram, GX_GY)
    factor = upper_factor(gram)
    upper_inv = lower_inverse(factor.T).T
    modes = jnp.dot(coarse_rows.astype(jnp.float32), upper_inv, precision=lax.Precision.HIGHEST)
    return (factor, modes.astype(jnp.bfloat16))


def solution(mesh):
    finer = Mesh(mesh.devices.reshape(4, 4, 4, 2), ("gx_0", "gx_1", "gy_0", "gy_1"))
    return jax.shard_map(
        shards,
        mesh=finer,
        in_specs=(P(GX_GY, None, None, None), P(GX_GY), P(GX_GY, None)),
        out_specs=(P(), P(GX_GY, None)),
        check_vma=False,
    )
```

profile of v0, /device:TPU:1, one launch (start us, length us, event | category | flops | bytes accessed | tf_op | source)
XLA Modules:
  0.0 594.9 jit_solution(3896506524874999614)
XLA Ops:
  7.2 9.0 %convert_reduce_fusion = f32[32,256,128]{2,1,0:T(8,128)S(1)} fusion(bf16[32,8,256,128]{3,2,1,0:T(8,128)(2,1)} %param.7), kind=kLoop, calls=%fused_computation.31 | loop fusion | flops 15728640 | bytes 20971520 | tf_op jit(solution)/shard_map/reduce_sum | solution.py:25
  16.8 1.0 constant_dynamic-slice_fusion
  17.8 1.4 collective-permute-start
  21.8 2.0 gather_fusion.2
  23.8 1.5 fusion.21
  25.4 41.4 %all-reduce.5.cloned.1.call-done = f32[128,128]{1,0:T(8,128)} async-done(((f32[128,128]{1,0:T(8,128)}), f32[128,128]{1,0:T(8,128)}) %all-reduce.5.cloned.1.call-update) | async-done | bytes 65552 | tf_op jit(solution)/shard_map/psum | solution.py:21
  67.1 43.6 %all-reduce.7.cloned.1.call-done = f32[128,128]{1,0:T(8,128)} async-done(((f32[128,128]{1,0:T(8,128)}), f32[128,128]{1,0:T(8,128)}) %all-reduce.7.cloned.1.call-update) | async-done | bytes 65552 | tf_op jit(solution)/shard_map/psum | solution.py:21
  110.8 44.1 %all-reduce.9.cloned.1.call-done = f32[128,128]{1,0:T(8,128)} async-done(((f32[128,128]{1,0:T(8,128)}), f32[128,128]{1,0:T(8,128)}) %all-reduce.9.cloned.1.call-update) | async-done | bytes 65552 | tf_op jit(solution)/shard_map/psum | solution.py:21
  154.9 3.4 fusion.22
  158.3 24.8 %all-reduce.11.cloned.1.call-done = f32[128,128]{1,0:T(8,128)} async-done(((f32[128,128]{1,0:T(8,128)}), f32[128,128]{1,0:T(8,128)}) %all-reduce.11.cloned.1.call-update) | async-done | bytes 65552 | tf_op jit(solution)/shard_map/psum | solution.py:21
  183.1 0.9 copy.9
  184.0 209.5 %while.30 = (s32[]{:T(128)}, f32[128,128]{1,0:T(8,128)S(1)}, f32[128,128]{0,1:T(8,128)S(1)}, s32[]{:T(128)}, s32[]{:T(128)}) while((s32[]{:T(128)}, f32[128,128]{1,0:T(8,128)S(1)}, f32[128,128]{0,1:T(8,128)S(1)}, s32[]{:T(128)}, s32[]{:T(128)}) %tuple.74), condition=%wide.region_6.7_spmd.clone.clone, body=%wide.region_5.6_spmd.clone.clone.sunk | while | flops 263171 | bytes 332904 | solution.py:52
  394.3 192.1 %while.31 = (s32[]{:T(128)}, f32[128,128]{1,0:T(8,128)S(1)}, f32[128,128]{1,0:T(8,128)S(1)}, f32[128,128]{1,0:T(8,128)S(1)}, s32[]{:T(128)}, /*index=5*/s32[]{:T(128)}) while((s32[]{:T(128)}, f32[128,128]{1,0:T(8,128)S(1)}, f32[128,128]{1,0:T(8,128)S(1)}, f32[128,128]{1,0:T(8,128)S(1)}, s32[]{:T(128)}, ...), condition=%wide.region_8.9_spmd.clone.clone, body=%wide.region_7.8_spmd.clone.clone.sunk | while | flops 262915 | bytes 201824 | solution.py:68
  396.4 0.8 fusion.49
  397.9 0.8 fusion.49
  399.4 0.8 fusion.49
  400.9 0.8 fusion.49
  402.4 0.8 fusion.49
  403.9 0.8 fusion.49
  405.4 0.8 fusion.49
  406.9 0.8 fusion.49
  408.4 0.8 fusion.49
  409.9 0.8 fusion.49
  586.4 2.0 convolution_convert_fusion
  (1303 shorter events, 302.5 us)
Async XLA Ops:
  7.2 59.6 %all-reduce.5.cloned.1.call-start = ((), (), s32[]{:S(2)}) async-start(), calls=%async_computation | async-start | bytes 131072 | tf_op jit(solution)/shard_map/psum | solution.py:21
  16.2 3.6 copy-start
  17.8 4.0 collective-permute-start
  25.3 85.4 %all-reduce.7.cloned.1.call-start = ((), (), s32[]{:S(2)}) async-start(), calls=%async_computation.1 | async-start | bytes 131072 | tf_op jit(solution)/shard_map/psum | solution.py:21
  66.8 88.1 %all-reduce.9.cloned.1.call-start = ((), (), s32[]{:S(2)}) async-start(), calls=%async_computation.2 | async-start | bytes 131072 | tf_op jit(solution)/shard_map/psum | solution.py:21
  110.7 72.4 %all-reduce.11.cloned.1.call-start = ((), (), s32[]{:S(2)}) async-start(), calls=%async_computation.3 | async-start | bytes 131072 | tf_op jit(solution)/shard_map/psum | solution.py:21
Sparse Core Ops, SparseCore 0:
  25.5 41.2 all-reduce.4
  69.1 41.5 all-reduce.6
  113.0 41.7 all-reduce.8
  157.1 25.9 all-reduce.10
where the time goes:
time: 597 us; the launch traced here: 595 us
  local copies, waits for them, and re-layouts  165 us (28%)
  waiting for transfers between devices  154 us (26%)
  matrix products  125 us (21%)
  loops' own time  95 us (16%)
  other arithmetic  39.5 us (7%)
  between operations  14.6 us (2%)
    psum x4, waiting for transfers between devices, by_axis(): return functools.reduce(lax.psum, axes, x)  154 us
    dot_general x128, matrix products, row_step(): jnp.dot(known, inverse, precision=lax.Precision.HIGHEST)  98.8 us
    another operation x1, loops' own time, lower_factor(): lax.fori_loop(0, width, column_step, jnp.zeros((width, width), jnp.float32))  91.4 us
    dynamic_slice x128, local copies, waits for them, and re-layouts, column_step(): pivot = jnp.sqrt(partial_col[column])  82.6 us
    dynamic_slice x128, local copies, waits for them, and re-layouts, row_step(): lower[row, row]  76.4 us
    dot_general x128, matrix products, column_step(): jnp.dot(lower, lower[column], precision=lax.Precision.HIGHEST)  22.4 us
    add x128, other arithmetic, row_step(): return inverse + marker[:, None] * values[None, :]  12.9 us
  transfers between devices with their start and end apart: 5, of which 5 were waited for; matrix products, arithmetic and copies ran while one was open for 1% of the time, Pallas kernels for 0%

commit v1 on v0

v1 whole, which is shorter than its diff:
```python
import functools

import jax
import jax.numpy as jnp
from jax import lax
from jax.experimental import pallas as pl
from jax.experimental.pallas import tpu as pltpu
from jax.sharding import Mesh
from jax.sharding import PartitionSpec as P

ALL = ("x", "y", "z", "c")
TILE = 8


def parity_of():
    return lax.axis_index("c")


def front_kernel(scale, count_ref, fine_ref, avg_ref, out_ref, keep_ref, send_ref, buf, acc, sems):
    slots, children, cells, width = buf.shape
    half = slots // 2
    parity = parity_of()
    count = count_ref[0]

    def load(slot):
        return pltpu.make_async_copy(fine_ref.at[slot], buf.at[slot], sems.at[slot])

    def start(k, _):
        load(k).start()
        load(k + half).start()
        return 0

    lax.fori_loop(0, half, start, 0)
    acc[...] = jnp.zeros_like(acc)
    rows = 32

    def averaged(slot):
        for first in range(0, cells, rows):
            total = buf[slot, 0, first : first + rows, :].astype(jnp.float32)
            for child in range(1, children):
                total += buf[slot, child, first : first + rows, :].astype(jnp.float32)
            avg_ref[slot, first : first + rows, :] = (total * (1.0 / children)).astype(jnp.bfloat16)

    def cross(slot):
        value = avg_ref[slot]
        held = jnp.where(slot < count, value, jnp.zeros_like(value))
        return lax.dot_general(held, value, (((0,), (0,)), ((), ())), preferred_element_type=jnp.float32)

    def body(k, _):
        load(k).wait()
        averaged(k)
        load(k + half).wait()
        averaged(k + half)
        out_ref[k] = jnp.where(parity == 0, avg_ref[k + half], avg_ref[k])
        acc[...] += cross(k) + cross(k + half)
        return 0

    lax.fori_loop(0, half, body, 0)
    top = acc[: width // 2, :] * scale
    low = acc[width // 2 :, :] * scale
    keep_ref[...] = jnp.where(parity == 0, top, low)
    send_ref[...] = jnp.where(parity == 0, low, top)


def lane_spread(tile, lane):
    return jnp.broadcast_to(tile[:, lane : lane + 1], tile.shape)


def row_spread(tile, row):
    return jnp.broadcast_to(tile[row : row + 1, :], tile.shape)


def eliminate(rows):
    shape = rows[0].shape
    lane = lax.broadcasted_iota(jnp.int32, shape, 1)
    sub = lax.broadcasted_iota(jnp.int32, shape, 0)
    rows = list(rows)
    factor, inverse = [], []
    for t in range(len(rows)):
        base = t * TILE
        inside = (lane >= base) & (lane < base + TILE)
        panel = rows[t]
        columns = [lane_spread(panel, base + c) for c in range(TILE)]
        d = [[row_spread(columns[c], i) for c in range(i + 1)] for i in range(TILE)]
        upper = [row_spread(panel, i) for i in range(TILE)]
        mixed = [jnp.where(inside, (lane == base + i).astype(jnp.float32), upper[i]) for i in range(TILE)]
        inv = [None] * TILE
        for r in range(TILE):
            inv[r] = lax.rsqrt(d[r][r])
            for i in range(r + 1, TILE):
                d[i][r] = d[i][r] * inv[r]
            mixed[r] = mixed[r] * inv[r]
            upper[r] = upper[r] * inv[r]
            for i in range(r + 1, TILE):
                for c in range(r + 1, i + 1):
                    d[i][c] = d[i][c] - d[i][r] * d[c][r]
                mixed[i] = mixed[i] - d[i][r] * mixed[r]
                upper[i] = upper[i] - d[i][r] * upper[r]
        for j in range(t + 1, len(rows)):
            b = [lane_spread(rows[j], base + c) for c in range(TILE)]
            z = jnp.where(inside, 0.0, rows[j])
            for r in range(TILE):
                b[r] = b[r] * inv[r]
                for c in range(r + 1, TILE):
                    b[c] = b[c] - b[r] * d[c][r]
                z = z - b[r] * mixed[r]
            rows[j] = z
        f, m = jnp.zeros(shape, jnp.float32), jnp.zeros(shape, jnp.float32)
        for r in range(TILE):
            f = jnp.where((sub == r) & (lane >= base + r), upper[r], f)
            m = jnp.where((sub == r) & (lane <= base + r), mixed[r], m)
        factor.append(f)
        inverse.append(m)
    return factor, inverse


def back_kernel(
    count_ref, place_ref, mine_ref, other_ref, own_ref, moved_ref, factor_ref, modes_ref, gram, inv, buf, out, in_sems, out_sems
):
    blocks, cells, width = out.shape
    slots = buf.shape[0] - blocks
    parity = parity_of()
    count = count_ref[0]
    loads = (
        pltpu.make_async_copy(own_ref, buf.at[pl.ds(0, slots)], in_sems.at[0]),
        pltpu.make_async_copy(moved_ref, buf.at[pl.ds(slots, blocks)], in_sems.at[1]),
    )
    for load in loads:
        load.start()
    mine, other = mine_ref[...], other_ref[...]
    gram[: width // 2, :] = jnp.where(parity == 0, mine, other)
    gram[width // 2 :, :] = jnp.where(parity == 0, other, mine)
    factor, inverse = eliminate([gram[i : i + TILE, :] for i in range(0, width, TILE)])
    for t in range(width // TILE):
        factor_ref[t * TILE : (t + 1) * TILE, :] = factor[t]
        inv[t * TILE : (t + 1) * TILE, :] = inverse[t]
    for load in loads:
        load.wait()
    rest = inv[...]
    parts = []
    for _ in range(3):
        part = rest.astype(jnp.bfloat16)
        parts.append(part)
        rest = rest - part.astype(jnp.float32)

    def store(i):
        return pltpu.make_async_copy(out.at[i], modes_ref.at[pl.ds(i * cells, cells)], out_sems.at[i])

    for i in range(blocks):
        wanted = place_ref[i]
        excess = blocks - count
        from_even = jnp.where(wanted < count, wanted, slots + wanted - count)
        from_odd = jnp.where(wanted < excess, slots + wanted, wanted - excess)
        index = jnp.where(parity == 0, from_even, from_odd)
        value = buf[index]
        total = jnp.zeros((cells, width), jnp.float32)
        for part in reversed(parts):
            total += lax.dot_general(value, part, (((1,), (1,)), ((), ())), preferred_element_type=jnp.float32)
        out[i] = total.astype(jnp.bfloat16)
        store(i).start()
    for i in range(blocks):
        store(i).wait()


def spread_sum(value, axes, members):
    sent = jnp.broadcast_to(value[None], (members,) + value.shape)
    return jnp.sum(lax.all_to_all(sent, axes, 0, 0), axis=0)


def swapped(value):
    return lax.ppermute(value, "c", [(0, 1), (1, 0)])


def shards(fine, patch_count, block_place):
    slots, children, cells, width = fine.shape
    blocks = slots // 2
    devices = 1
    for axis in ALL:
        devices *= lax.axis_size(axis)
    row_total = blocks * cells * devices
    vmem, smem, hbm = pltpu.VMEM, pltpu.SMEM, pl.ANY
    spec = lambda space: pl.BlockSpec(memory_space=space)
    own, outgoing, keep, send = pl.pallas_call(
        functools.partial(front_kernel, 1.0 / row_total),
        out_shape=(
            jax.ShapeDtypeStruct((slots, cells, width), jnp.bfloat16),
            jax.ShapeDtypeStruct((blocks, cells, width), jnp.bfloat16),
            jax.ShapeDtypeStruct((width // 2, width), jnp.float32),
            jax.ShapeDtypeStruct((width // 2, width), jnp.float32),
        ),
        in_specs=[spec(smem), spec(hbm)],
        out_specs=[spec(vmem)] * 4,
        scratch_shapes=[
            pltpu.VMEM(fine.shape, jnp.bfloat16),
            pltpu.VMEM((width, width), jnp.float32),
            pltpu.SemaphoreType.DMA((slots,)),
        ],
        compiler_params=pltpu.CompilerParams(vmem_limit_bytes=50 * 2**20),
        name="front",
    )(patch_count, fine)
    half = keep + swapped(send)
    moved = swapped(outgoing)
    half = spread_sum(half, ("x", "y"), lax.axis_size("x") * lax.axis_size("y"))
    half = spread_sum(half, ("z",), lax.axis_size("z"))
    other = swapped(half)
    factor, modes = pl.pallas_call(
        back_kernel,
        out_shape=(
            jax.ShapeDtypeStruct((width, width), jnp.float32),
            jax.ShapeDtypeStruct((blocks * cells, width), jnp.bfloat16),
        ),
        in_specs=[spec(smem), spec(smem), spec(vmem), spec(vmem), spec(pl.ANY), spec(pl.ANY)],
        out_specs=[spec(vmem), spec(hbm)],
        scratch_shapes=[
            pltpu.VMEM((width, width), jnp.float32),
            pltpu.VMEM((width, width), jnp.float32),
            pltpu.VMEM((slots + blocks, cells, width), jnp.bfloat16),
            pltpu.VMEM((blocks, cells, width), jnp.bfloat16),
            pltpu.SemaphoreType.DMA((2,)),
            pltpu.SemaphoreType.DMA((blocks,)),
        ],
        compiler_params=pltpu.CompilerParams(vmem_limit_bytes=20 * 2**20),
        name="back",
    )(patch_count, block_place.reshape(-1), half, other, own, moved)
    return (factor, modes)


def solution(mesh):
    sizes = mesh.shape
    finer = Mesh(mesh.devices.reshape(4, sizes["gx"] // 4, sizes["gy"] // 2, 2), ALL)
    return jax.shard_map(
        shards,
        mesh=finer,
        in_specs=(P(ALL, None, None, None), P(ALL), P(ALL, None)),
        out_specs=(P(), P(ALL, None)),
        check_vma=False,
    )
```

time: 597 us -> 53.5 us (0.09)
  local copies, waits for them, and re-layouts: 165 us -> 0.06 us
  waiting for transfers between devices: 154 us -> 3.31 us
  matrix products: 125 us -> 0 us
  loops' own time: 95 us -> 0 us
  other arithmetic: 39.5 us -> 1.1 us
  blocking collectives: 0 us -> 26.8 us
  Pallas kernels: 0 us -> 15.5 us
  between operations: 14.6 us -> 1.33 us
    dynamic_slice x257 -> x0, local copies, waits for them, and re-layouts: 160 us -> none  [the longest x128 82.6 us: column_step(): pivot = jnp.sqrt(partial_col[column])]
    psum x4 -> x0, waiting for transfers between devices: 154 us -> none  [by_axis(): return functools.reduce(lax.psum, axes, x)]
    dot_general x258 -> x0, matrix products: 125 us -> none  [the longest x128 98.8 us: row_step(): jnp.dot(known, inverse, precision=lax.Precision.HIGHEST)]
    another operation x2 -> x0, loops' own time: 95 us -> none  [the longest x1 91.4 us: lower_factor(): lax.fori_loop(0, width, column_step, jnp.zeros((width, width), jnp.float32))]
    all_to_all x0 -> x2, blocking collectives: none -> 26.8 us  [spread_sum(): return jnp.sum(lax.all_to_all(sent, axes, 0, 0), axis=0)]
    add x256 -> x1, other arithmetic: 23.7 us -> 0.01 us  [shards(): half = keep + swapped(send)]
    pallas_call x0 -> x2, Pallas kernels: none -> 15.5 us  [the longest x1 8.42 us: shards(): pl.pallas_call(functools.partial(front_kernel, 1.0 / row_total), out_shap...]
    reduce_sum x1 -> x2, other arithmetic: 9.01 us -> 1.09 us  [spread_sum(): return jnp.sum(lax.all_to_all(sent, axes, 0, 0), axis=0)]
  transfers between devices with their start and end apart: 5 -> 3, of which waited for: 5 -> 2; matrix products, arithmetic and copies ran while one was open for 1% -> 2% of each run, Pallas kernels for 0% -> 0%
where the time goes in v1:
time: 53.5 us; the launch traced here: 53.2 us
  blocking collectives  26.8 us (50%)
  Pallas kernels  15.5 us (29%)
  starting transfers between devices  5.13 us (10%)
  waiting for transfers between devices  3.31 us (6%)
  between operations  1.33 us (2%)
  other arithmetic  1.1 us (2%)
    all_to_all x2, blocking collectives, spread_sum(): return jnp.sum(lax.all_to_all(sent, axes, 0, 0), axis=0)  26.8 us
    pallas_call x1, Pallas kernels, shards(): pl.pallas_call(functools.partial(front_kernel, 1.0 / row_total), out_shap...  8.42 us
    pallas_call x1, Pallas kernels, shards(): pl.pallas_call(back_kernel, out_shape=(jax.ShapeDtypeStruct((width, width...  7.06 us
    ppermute x3, starting transfers between devices, swapped(): return lax.ppermute(value, 'c', [(0, 1), (1, 0)])  5.13 us
    ppermute x3, waiting for transfers between devices, swapped(): return lax.ppermute(value, 'c', [(0, 1), (1, 0)])  3.31 us
    reduce_sum x2, other arithmetic, spread_sum(): return jnp.sum(lax.all_to_all(sent, axes, 0, 0), axis=0)  1.09 us
  transfers between devices with their start and end apart: 3, of which 2 were waited for; matrix products, arithmetic and copies ran while one was open for 2% of the time, Pallas kernels for 0%

profile of v1, /device:TPU:1, one launch (start us, length us, event | category | flops | bytes accessed | tf_op | source)
XLA Modules:
  0.0 53.2 jit_solution(8398799289364983856)
XLA Ops:
  0.6 0.0 copy-start
  1.3 8.4 %front.1 = (bf16[32,256,128]{2,1,0:T(8,128)(2,1)S(1)}, bf16[16,256,128]{2,1,0:T(8,128)(2,1)}, f32[64,128]{1,0:T(8,128)S(1)}, f32[64,128]{1,0:T(8,128)S(1)}) custom-call(s32[1]{0:T(128)S(6)} %copy.5.count_ref, bf16[32,8,256,128]{3,2,1,0:T(8,128)(2,1)} %fine_ref.1), custom_call_target="tpu_custom_call" | custom-call | tf_op jit(solution)/shard_map/front/pallas_call | solution.py:183
  9.7 1.5 %collective-permute-start.2 = (bf16[16,256,128]{2,1,0:T(8,128)(2,1)}, bf16[16,256,128]{2,1,0:T(8,128)(2,1)S(1)}, u32[]{:S(2)}, u32[]{:S(2)}) collective-permute-start(bf16[16,256,128]{2,1,0:T(8,128)(2,1)} %get-tuple-element.9), channel_id=1, source_target_pairs={{0,1},{1,0},{2,3},{3,2},{4,5},{5,4},{6,7},{7,6},{8,9},{9,8},{10,11... | collective-permute-start | bytes 3145736 | tf_op jit(solution)/shard_map/ppermute | solution.py:171
  11.2 0.1 collective-permute-start
  11.3 2.5 %collective-permute-done = f32[64,128]{1,0:T(8,128)S(1)} collective-permute-done((f32[64,128]{1,0:T(8,128)S(1)}, f32[64,128]{1,0:T(8,128)S(1)}, u32[]{:S(2)}, u32[]{:S(2)}) %collective-permute-start) | collective-permute-done | bytes 32800 | tf_op jit(solution)/shard_map/ppermute | solution.py:171
  13.8 17.1 %all_to_all.10 = f32[16,64,128]{2,1,0:T(8,128)} all-to-all(f32[16,64,128]{2,1,0:T(8,128)S(1)} %broadcast_in_dim.4), channel_id=1, replica_groups=mesh['x'=4,'y'=4,'z'=4,'c'=2] {'x','y'}, dimensions={0} | all-to-all | bytes 1048576 | tf_op jit(solution)/shard_map/all_to_all | solution.py:167
  30.9 1.1 %reduce_sum.18 = f32[64,128]{1,0:T(8,128)S(1)} reduce(f32[16,64,128]{2,1,0:T(8,128)} %all_to_all.10, f32[]{:T(128)} %constant.0.clone.1), dimensions={0}, to_apply=%region_0.0 | reduce | flops 122880 | bytes 557060 | tf_op jit(solution)/shard_map/reduce_sum | solution.py:167
  32.0 9.7 %all_to_all.11 = f32[4,64,128]{2,1,0:T(8,128)S(1)} all-to-all(f32[4,64,128]{2,1,0:T(8,128)S(1)} %broadcast_in_dim.5), channel_id=1, replica_groups=mesh['x'=4,'y'=4,'z'=4,'c'=2] {'z'}, dimensions={0} | all-to-all | bytes 262144 | tf_op jit(solution)/shard_map/all_to_all | solution.py:167
  41.7 3.6 %collective-permute-start.1 = (f32[64,128]{1,0:T(8,128)S(1)}, f32[64,128]{1,0:T(8,128)S(1)}, u32[]{:S(2)}, u32[]{:S(2)}) collective-permute-start(f32[64,128]{1,0:T(8,128)S(1)} %reduce_sum.19.mine_ref), channel_id=1, source_target_pairs={{0,1},{1,0},{2,3},{3,2},{4,5},{5,4},{6,7},{7,6},{8,9},{9,8},{10,11... | collective-permute-start | bytes 98312 | tf_op jit(solution)/shard_map/ppermute | solution.py:171
  45.3 0.9 %collective-permute-done.1.other_ref = f32[64,128]{1,0:T(8,128)S(1)} collective-permute-done((f32[64,128]{1,0:T(8,128)S(1)}, f32[64,128]{1,0:T(8,128)S(1)}, u32[]{:S(2)}, u32[]{:S(2)}) %collective-permute-start.1) | collective-permute-done | bytes 32800 | tf_op jit(solution)/shard_map/ppermute | solution.py:171
  46.1 0.0 collective-permute-done.2.moved_ref
  46.1 0.0 copy-done
  46.2 7.1 %back.1 = (f32[128,128]{1,0:T(8,128)}, bf16[4096,128]{1,0:T(8,128)(2,1)}) custom-call(s32[1]{0:T(128)S(6)} %copy.5.count_ref, s32[16]{0:T(128)S(1)} %bitcast.1, f32[64,128]{1,0:T(8,128)S(1)} %reduce_sum.19.mine_ref, f32[64,128]{1,0:T(8,128)S(1)} %collective-permute-done.1.other_ref, bf16[32,256,128]{2,1,0:T(8,128)(2,1)S(1)} %get-tuple-element.8.own_ref, ...), custom_call_target="tpu_custom_call" | custom-call | tf_op jit(solution)/shard_map/back/pallas_call | solution.py:206
  (4 shorter events, 0.1 us)
Async XLA Ops:
  0.6 45.5 %copy-start = (s32[1,16]{1,0:T(1,128)S(1)}, s32[1,16]{1,0:T(1,128)}, u32[]{:S(2)}) copy-start(s32[1,16]{1,0:T(1,128)} %param.5) | copy-start | bytes 196
  9.7 36.4 %collective-permute-start.2 = (bf16[16,256,128]{2,1,0:T(8,128)(2,1)}, bf16[16,256,128]{2,1,0:T(8,128)(2,1)S(1)}, u32[]{:S(2)}, u32[]{:S(2)}) collective-permute-start(bf16[16,256,128]{2,1,0:T(8,128)(2,1)} %get-tuple-element.9), channel_id=1, source_target_pairs={{0,1},{1,0},{2,3},{3,2},{4,5},{5,4},{6,7},{7,6},{8,9},{9,8},{10,11... | collective-permute-start | bytes 3145736 | tf_op jit(solution)/shard_map/ppermute | solution.py:171
  11.2 2.5 %collective-permute-start = (f32[64,128]{1,0:T(8,128)S(1)}, f32[64,128]{1,0:T(8,128)S(1)}, u32[]{:S(2)}, u32[]{:S(2)}) collective-permute-start(f32[64,128]{1,0:T(8,128)S(1)} %get-tuple-element.7), channel_id=1, source_target_pairs={{0,1},{1,0},{2,3},{3,2},{4,5},{5,4},{6,7},{7,6},{8,9},{9,8},{10,11... | collective-permute-start | bytes 98312 | tf_op jit(solution)/shard_map/ppermute | solution.py:171
  41.7 4.4 %collective-permute-start.1 = (f32[64,128]{1,0:T(8,128)S(1)}, f32[64,128]{1,0:T(8,128)S(1)}, u32[]{:S(2)}, u32[]{:S(2)}) collective-permute-start(f32[64,128]{1,0:T(8,128)S(1)} %reduce_sum.19.mine_ref), channel_id=1, source_target_pairs={{0,1},{1,0},{2,3},{3,2},{4,5},{5,4},{6,7},{7,6},{8,9},{9,8},{10,11... | collective-permute-start | bytes 98312 | tf_op jit(solution)/shard_map/ppermute | solution.py:171

commit v2 on v1

--- a/solution.py
+++ b/solution.py
@@ -16,50 +16,92 @@
     return lax.axis_index("c")
 
 
-def front_kernel(scale, count_ref, fine_ref, avg_ref, out_ref, keep_ref, send_ref, buf, acc, sems):
+def front_kernel(
+    scale, groups, count_hbm, fine_ref, avg_ref, out_hbm, keep_ref, send_ref, buf, acc, count_ref, sems, out_sems, count_sem
+):
     slots, children, cells, width = buf.shape
     half = slots // 2
     parity = parity_of()
-    count = count_ref[0]
 
     def load(slot):
         return pltpu.make_async_copy(fine_ref.at[slot], buf.at[slot], sems.at[slot])
 
+    load_count = pltpu.make_async_copy(count_hbm, count_ref, count_sem.at[0])
+    load_count.start()
+
+    def sent_slot(k):
+        return k + half * (1 - parity)
+
+    def other_slot(k):
+        return k + half * parity
+
     def start(k, _):
-        load(k).start()
-        load(k + half).start()
+        load(sent_slot(k)).start()
+        load(other_slot(k)).start()
         return 0
 
     lax.fori_loop(0, half, start, 0)
-    acc[...] = jnp.zeros_like(acc)
+    load_count.wait()
+    count = count_ref[0]
     rows = 32
 
+    def send_out(k):
+        return pltpu.make_async_copy(avg_ref.at[sent_slot(k)], out_hbm.at[k], out_sems.at[k])
+
     def averaged(slot):
+        factor = jnp.where(slot < count, 1.0 / children, 0.0)
         for first in range(0, cells, rows):
             total = buf[slot, 0, first : first + rows, :].astype(jnp.float32)
             for child in range(1, children):
                 total += buf[slot, child, first : first + rows, :].astype(jnp.float32)
-            avg_ref[slot, first : first + rows, :] = (total * (1.0 / children)).astype(jnp.bfloat16)
-
-    def cross(slot):
-        value = avg_ref[slot]
-        held = jnp.where(slot < count, value, jnp.zeros_like(value))
-        return lax.dot_general(held, value, (((0,), (0,)), ((), ())), preferred_element_type=jnp.float32)
+            avg_ref[slot, first : first + rows, :] = (total * factor).astype(jnp.bfloat16)
 
     def body(k, _):
-        load(k).wait()
-        averaged(k)
-        load(k + half).wait()
-        averaged(k + half)
-        out_ref[k] = jnp.where(parity == 0, avg_ref[k + half], avg_ref[k])
-        acc[...] += cross(k) + cross(k + half)
+        load(sent_slot(k)).wait()
+        averaged(sent_slot(k))
+        send_out(k).start()
+        load(other_slot(k)).wait()
+        averaged(other_slot(k))
         return 0
 
-    lax.fori_loop(0, half, body, 0)
-    top = acc[: width // 2, :] * scale
-    low = acc[width // 2 :, :] * scale
+    def cross(first, many):
+        value = avg_ref[first : first + many].reshape(many * cells, width)
+        return lax.dot_general(value, value, (((0,), (0,)), ((), ())), preferred_element_type=jnp.float32)
+
+    done = 0
+    for many in groups:
+        lax.fori_loop(done, done + many, body, 0)
+        part = cross(done, many) + cross(done + half, many)
+        acc[...] = part if done == 0 else acc[...] + part
+        done += many
+    lane = lax.broadcasted_iota(jnp.int32, (width // 4, width), 1)
+    strips = [acc[i : i + width // 4, :] * scale for i in range(0, width, width // 4)]
+    second = jnp.where(lane < width // 4, pltpu.roll(strips[3], width // 4, 1), strips[1])
+    cut = width // 8
+    third = jnp.where(lane[:cut] < width // 2, pltpu.roll(strips[2][cut:], width // 2, 1), strips[2][:cut])
+    packed = jnp.concatenate([strips[0], second, third], axis=0)
+    middle = packed.shape[0] // 2
+    top, low = packed[:middle], packed[middle:]
     keep_ref[...] = jnp.where(parity == 0, top, low)
     send_ref[...] = jnp.where(parity == 0, low, top)
+
+    def finish(k, _):
+        send_out(k).wait()
+        return 0
+
+    lax.fori_loop(0, half, finish, 0)
+
+
+def unpacked(packed):
+    width = packed.shape[1]
+    quarter, cut = width // 4, width // 8
+    second, third = packed[quarter : 2 * quarter], packed[2 * quarter :]
+    upper = jnp.concatenate(
+        [packed[: 2 * quarter], third, pltpu.roll(third, width // 2, 1), pltpu.roll(second, width - quarter, 1)], axis=0
+    )
+    row = lax.broadcasted_iota(jnp.int32, upper.shape, 0)
+    lane = lax.broadcasted_iota(jnp.int32, upper.shape, 1)
+    return jnp.where(lane // quarter >= row // quarter, upper, upper.T)
 
 
 def lane_spread(tile, lane):
@@ -115,27 +157,29 @@
 
 
 def back_kernel(
-    count_ref, place_ref, mine_ref, other_ref, own_ref, moved_ref, factor_ref, modes_ref, gram, inv, buf, out, in_sems, out_sems
+    count_hbm, place_hbm, mine_ref, other_ref, own_ref, moved_ref, factor_ref, modes_ref, gram, inv, buf, out, count_ref, place_ref, in_sems, out_sems
 ):
     blocks, cells, width = out.shape
     slots = buf.shape[0] - blocks
     parity = parity_of()
-    count = count_ref[0]
     loads = (
+        pltpu.make_async_copy(count_hbm, count_ref, in_sems.at[2]),
+        pltpu.make_async_copy(place_hbm, place_ref, in_sems.at[3]),
         pltpu.make_async_copy(own_ref, buf.at[pl.ds(0, slots)], in_sems.at[0]),
         pltpu.make_async_copy(moved_ref, buf.at[pl.ds(slots, blocks)], in_sems.at[1]),
     )
     for load in loads:
         load.start()
     mine, other = mine_ref[...], other_ref[...]
-    gram[: width // 2, :] = jnp.where(parity == 0, mine, other)
-    gram[width // 2 :, :] = jnp.where(parity == 0, other, mine)
+    packed = jnp.concatenate([jnp.where(parity == 0, mine, other), jnp.where(parity == 0, other, mine)], axis=0)
+    gram[...] = unpacked(packed)
     factor, inverse = eliminate([gram[i : i + TILE, :] for i in range(0, width, TILE)])
     for t in range(width // TILE):
         factor_ref[t * TILE : (t + 1) * TILE, :] = factor[t]
         inv[t * TILE : (t + 1) * TILE, :] = inverse[t]
     for load in loads:
         load.wait()
+    count = count_ref[0]
     rest = inv[...]
     parts = []
     for _ in range(3):
@@ -147,7 +191,7 @@
         return pltpu.make_async_copy(out.at[i], modes_ref.at[pl.ds(i * cells, cells)], out_sems.at[i])
 
     for i in range(blocks):
-        wanted = place_ref[i]
+        wanted = place_ref[0, i]
         excess = blocks - count
         from_even = jnp.where(wanted < count, wanted, slots + wanted - count)
         from_odd = jnp.where(wanted < excess, slots + wanted, wanted - excess)
@@ -171,6 +215,10 @@
     return lax.ppermute(value, "c", [(0, 1), (1, 0)])
 
 
+def groups_of(total):
+    return [total // 4] * 3 + [total // 4 - 1, 1]
+
+
 def shards(fine, patch_count, block_place):
     slots, children, cells, width = fine.shape
     blocks = slots // 2
@@ -178,27 +226,31 @@
     for axis in ALL:
         devices *= lax.axis_size(axis)
     row_total = blocks * cells * devices
-    vmem, smem, hbm = pltpu.VMEM, pltpu.SMEM, pl.ANY
+    vmem, hbm = pltpu.VMEM, pl.ANY
     spec = lambda space: pl.BlockSpec(memory_space=space)
     own, outgoing, keep, send = pl.pallas_call(
-        functools.partial(front_kernel, 1.0 / row_total),
+        functools.partial(front_kernel, 1.0 / row_total, groups_of(blocks)),
         out_shape=(
             jax.ShapeDtypeStruct((slots, cells, width), jnp.bfloat16),
             jax.ShapeDtypeStruct((blocks, cells, width), jnp.bfloat16),
-            jax.ShapeDtypeStruct((width // 2, width), jnp.float32),
-            jax.ShapeDtypeStruct((width // 2, width), jnp.float32),
+            jax.ShapeDtypeStruct((width * 5 // 16, width), jnp.float32),
+            jax.ShapeDtypeStruct((width * 5 // 16, width), jnp.float32),
         ),
-        in_specs=[spec(smem), spec(hbm)],
-        out_specs=[spec(vmem)] * 4,
+        in_specs=[spec(hbm), spec(hbm)],
+        out_specs=[spec(vmem), spec(hbm), spec(vmem), spec(vmem)],
         scratch_shapes=[
             pltpu.VMEM(fine.shape, jnp.bfloat16),
             pltpu.VMEM((width, width), jnp.float32),
+            pltpu.SMEM((1,), jnp.int32),
             pltpu.SemaphoreType.DMA((slots,)),
+            pltpu.SemaphoreType.DMA((blocks,)),
+            pltpu.SemaphoreType.DMA((1,)),
         ],
         compiler_params=pltpu.CompilerParams(vmem_limit_bytes=50 * 2**20),
         name="front",
     )(patch_count, fine)
     half = keep + swapped(send)
+    half, outgoing = lax.optimization_barrier((half, outgoing))
     moved = swapped(outgoing)
     half = spread_sum(half, ("x", "y"), lax.axis_size("x") * lax.axis_size("y"))
     half = spread_sum(half, ("z",), lax.axis_size("z"))
@@ -209,19 +261,21 @@
             jax.ShapeDtypeStruct((width, width), jnp.float32),
             jax.ShapeDtypeStruct((blocks * cells, width), jnp.bfloat16),
         ),
-        in_specs=[spec(smem), spec(smem), spec(vmem), spec(vmem), spec(pl.ANY), spec(pl.ANY)],
+        in_specs=[spec(hbm), spec(hbm), spec(vmem), spec(vmem), spec(hbm), spec(hbm)],
         out_specs=[spec(vmem), spec(hbm)],
         scratch_shapes=[
             pltpu.VMEM((width, width), jnp.float32),
             pltpu.VMEM((width, width), jnp.float32),
             pltpu.VMEM((slots + blocks, cells, width), jnp.bfloat16),
             pltpu.VMEM((blocks, cells, width), jnp.bfloat16),
-            pltpu.SemaphoreType.DMA((2,)),
+            pltpu.SMEM((1,), jnp.int32),
+            pltpu.SMEM((1, blocks), jnp.int32),
+            pltpu.SemaphoreType.DMA((4,)),
             pltpu.SemaphoreType.DMA((blocks,)),
         ],
         compiler_params=pltpu.CompilerParams(vmem_limit_bytes=20 * 2**20),
         name="back",
-    )(patch_count, block_place.reshape(-1), half, other, own, moved)
+    )(patch_count, block_place, half, other, own, moved)
     return (factor, modes)
 
 

time: 53.5 us -> 46.8 us (0.87)
  blocking collectives: 26.8 us -> 24.2 us
  waiting for transfers between devices: 3.31 us -> 1.69 us
  Pallas kernels: 15.5 us -> 14 us
  other arithmetic: 1.1 us -> 0.04 us
    all_to_all x2, blocking collectives: 26.8 us -> 24.2 us  [spread_sum(): return jnp.sum(lax.all_to_all(sent, axes, 0, 0), axis=0)]
    ppermute x3, waiting for transfers between devices: 3.31 us -> 1.69 us  [swapped(): return lax.ppermute(value, 'c', [(0, 1), (1, 0)])]
    pallas_call x1, Pallas kernels: 8.42 us -> 7.31 us  [shards(): pl.pallas_call(functools.partial(front_kernel, 1.0 / row_total, groups_of...]
    reduce_sum x2, other arithmetic: 1.09 us -> 0.03 us  [spread_sum(): return jnp.sum(lax.all_to_all(sent, axes, 0, 0), axis=0)]
  transfers between devices with their start and end apart: 3 -> 3, of which waited for: 2 -> 2; matrix products, arithmetic and copies ran while one was open for 2% -> 0% of each run, Pallas kernels for 0% -> 0%
where the time goes in v2:
time: 46.8 us; the launch traced here: 46.6 us
  blocking collectives  24.2 us (52%)
  Pallas kernels  14 us (30%)
  starting transfers between devices  5.27 us (11%)
  waiting for transfers between devices  1.69 us (4%)
  between operations  1.33 us (3%)
    all_to_all x2, blocking collectives, spread_sum(): return jnp.sum(lax.all_to_all(sent, axes, 0, 0), axis=0)  24.2 us
    pallas_call x1, Pallas kernels, shards(): pl.pallas_call(functools.partial(front_kernel, 1.0 / row_total, groups_of...  7.31 us
    pallas_call x1, Pallas kernels, shards(): pl.pallas_call(back_kernel, out_shape=(jax.ShapeDtypeStruct((width, width...  6.69 us
    ppermute x3, starting transfers between devices, swapped(): return lax.ppermute(value, 'c', [(0, 1), (1, 0)])  5.27 us
    ppermute x3, waiting for transfers between devices, swapped(): return lax.ppermute(value, 'c', [(0, 1), (1, 0)])  1.69 us
  transfers between devices with their start and end apart: 3, of which 2 were waited for; matrix products, arithmetic and copies ran while one was open for 0% of the time, Pallas kernels for 0%

profile of v2, /device:TPU:1, one launch (start us, length us, event | category | flops | bytes accessed | tf_op | source)
XLA Modules:
  0.0 46.6 jit_solution(938093562118255142)
XLA Ops:
  0.6 0.0 copy-start
  1.3 7.3 %front.1 = (bf16[32,256,128]{2,1,0:T(8,128)(2,1)S(1)}, bf16[16,256,128]{2,1,0:T(8,128)(2,1)}, f32[40,128]{1,0:T(8,128)S(1)}, f32[40,128]{1,0:T(8,128)S(1)}) custom-call(s32[1]{0:T(128)S(6)} %copy.5.count_hbm, bf16[32,8,256,128]{3,2,1,0:T(8,128)(2,1)} %fine_ref.1), custom_call_target="tpu_custom_call" | custom-call | tf_op jit(solution)/shard_map/front/pallas_call | solution.py:231
  8.6 1.5 %collective-permute-start = (f32[40,128]{1,0:T(8,128)S(1)}, f32[40,128]{1,0:T(8,128)S(1)}, u32[]{:S(2)}, u32[]{:S(2)}) collective-permute-start(f32[40,128]{1,0:T(8,128)S(1)} %get-tuple-element.9), channel_id=1, source_target_pairs={{0,1},{1,0},{2,3},{3,2},{4,5},{5,4},{6,7},{7,6},{8,9},{9,8},{10,11... | collective-permute-start | bytes 61448 | tf_op jit(solution)/shard_map/ppermute | solution.py:215
  10.1 0.8 %collective-permute-done = f32[40,128]{1,0:T(8,128)S(1)} collective-permute-done((f32[40,128]{1,0:T(8,128)S(1)}, f32[40,128]{1,0:T(8,128)S(1)}, u32[]{:S(2)}, u32[]{:S(2)}) %collective-permute-start) | collective-permute-done | bytes 20512 | tf_op jit(solution)/shard_map/ppermute | solution.py:215
  10.9 0.3 collective-permute-start.2
  11.3 14.8 %all_to_all.10 = f32[16,40,128]{2,1,0:T(8,128)S(1)} all-to-all(f32[16,40,128]{2,1,0:T(8,128)S(1)} %broadcast_in_dim.4), channel_id=1, replica_groups=mesh['x'=4,'y'=4,'z'=4,'c'=2] {'x','y'}, dimensions={0} | all-to-all | bytes 655360 | tf_op jit(solution)/shard_map/all_to_all | solution.py:211
  26.2 9.4 %all_to_all.11 = f32[4,40,128]{2,1,0:T(8,128)S(1)} all-to-all(f32[4,40,128]{2,1,0:T(8,128)S(1)} %broadcast_in_dim.5), channel_id=1, replica_groups=mesh['x'=4,'y'=4,'z'=4,'c'=2] {'z'}, dimensions={0} | all-to-all | bytes 163840 | tf_op jit(solution)/shard_map/all_to_all | solution.py:211
  35.6 3.5 %collective-permute-start.1 = (f32[40,128]{1,0:T(8,128)S(1)}, f32[40,128]{1,0:T(8,128)S(1)}, u32[]{:S(2)}, u32[]{:S(2)}) collective-permute-start(f32[40,128]{1,0:T(8,128)S(1)} %reduce_sum.19.mine_ref), channel_id=1, source_target_pairs={{0,1},{1,0},{2,3},{3,2},{4,5},{5,4},{6,7},{7,6},{8,9},{9,8},{10,11... | collective-permute-start | bytes 61448 | tf_op jit(solution)/shard_map/ppermute | solution.py:215
  39.0 0.8 %collective-permute-done.1.other_ref = f32[40,128]{1,0:T(8,128)S(1)} collective-permute-done((f32[40,128]{1,0:T(8,128)S(1)}, f32[40,128]{1,0:T(8,128)S(1)}, u32[]{:S(2)}, u32[]{:S(2)}) %collective-permute-start.1) | collective-permute-done | bytes 20512 | tf_op jit(solution)/shard_map/ppermute | solution.py:215
  39.9 0.0 collective-permute-done.2.moved_ref
  39.9 0.0 copy-done
  39.9 6.7 %back.1 = (f32[128,128]{1,0:T(8,128)}, bf16[4096,128]{1,0:T(8,128)(2,1)}) custom-call(s32[1]{0:T(128)S(6)} %copy.5.count_hbm, s32[1,16]{1,0:T(1,128)S(1)} %copy-done, f32[40,128]{1,0:T(8,128)S(1)} %reduce_sum.19.mine_ref, f32[40,128]{1,0:T(8,128)S(1)} %collective-permute-done.1.other_ref, bf16[32,256,128]{2,1,0:T(8,128)(2,1)S(1)} %get-tuple-element.12.own_ref, ...), custom_call_target="tpu_custom_call" | custom-call | tf_op jit(solution)/shard_map/back/pallas_call | solution.py:258
  (5 shorter events, 0.1 us)
Async XLA Ops:
  0.6 39.3 %copy-start = (s32[1,16]{1,0:T(1,128)S(1)}, s32[1,16]{1,0:T(1,128)}, u32[]{:S(2)}) copy-start(s32[1,16]{1,0:T(1,128)} %place_hbm.1) | copy-start | bytes 196
  8.6 2.3 %collective-permute-start = (f32[40,128]{1,0:T(8,128)S(1)}, f32[40,128]{1,0:T(8,128)S(1)}, u32[]{:S(2)}, u32[]{:S(2)}) collective-permute-start(f32[40,128]{1,0:T(8,128)S(1)} %get-tuple-element.9), channel_id=1, source_target_pairs={{0,1},{1,0},{2,3},{3,2},{4,5},{5,4},{6,7},{7,6},{8,9},{9,8},{10,11... | collective-permute-start | bytes 61448 | tf_op jit(solution)/shard_map/ppermute | solution.py:215
  10.9 29.0 %collective-permute-start.2 = (bf16[16,256,128]{2,1,0:T(8,128)(2,1)}, bf16[16,256,128]{2,1,0:T(8,128)(2,1)S(1)}, u32[]{:S(2)}, u32[]{:S(2)}) collective-permute-start(bf16[16,256,128]{2,1,0:T(8,128)(2,1)} %get-tuple-element.13), channel_id=1, source_target_pairs={{0,1},{1,0},{2,3},{3,2},{4,5},{5,4},{6,7},{7,6},{8,9},{9,8},{10,11... | collective-permute-start | bytes 3145736 | tf_op jit(solution)/shard_map/ppermute | solution.py:215
  35.6 4.3 %collective-permute-start.1 = (f32[40,128]{1,0:T(8,128)S(1)}, f32[40,128]{1,0:T(8,128)S(1)}, u32[]{:S(2)}, u32[]{:S(2)}) collective-permute-start(f32[40,128]{1,0:T(8,128)S(1)} %reduce_sum.19.mine_ref), channel_id=1, source_target_pairs={{0,1},{1,0},{2,3},{3,2},{4,5},{5,4},{6,7},{7,6},{8,9},{9,8},{10,11... | collective-permute-start | bytes 61448 | tf_op jit(solution)/shard_map/ppermute | solution.py:215

commit v3 on v2

--- a/solution.py
+++ b/solution.py
@@ -17,7 +17,7 @@
 
 
 def front_kernel(
-    scale, groups, count_hbm, fine_ref, avg_ref, out_hbm, keep_ref, send_ref, buf, acc, count_ref, sems, out_sems, count_sem
+    scale, groups, count_hbm, fine_ref, avg_ref, out_hbm, part_ref, buf, acc, count_ref, sems, out_sems, count_sem
 ):
     slots, children, cells, width = buf.shape
     half = slots // 2
@@ -29,24 +29,21 @@
     load_count = pltpu.make_async_copy(count_hbm, count_ref, count_sem.at[0])
     load_count.start()
 
-    def sent_slot(k):
-        return k + half * (1 - parity)
-
-    def other_slot(k):
-        return k + half * parity
-
-    def start(k, _):
-        load(sent_slot(k)).start()
-        load(other_slot(k)).start()
+    first_sent = half * (1 - parity)
+    first_kept = half * parity
+
+    def start(k, _, first):
+        load(first + k).start()
         return 0
 
-    lax.fori_loop(0, half, start, 0)
+    for first in (first_sent, first_kept):
+        lax.fori_loop(0, half, functools.partial(start, first=first), 0)
     load_count.wait()
     count = count_ref[0]
     rows = 32
 
     def send_out(k):
-        return pltpu.make_async_copy(avg_ref.at[sent_slot(k)], out_hbm.at[k], out_sems.at[k])
+        return pltpu.make_async_copy(avg_ref.at[first_sent + k], out_hbm.at[k], out_sems.at[k])
 
     def averaged(slot):
         factor = jnp.where(slot < count, 1.0 / children, 0.0)
@@ -56,34 +53,34 @@
                 total += buf[slot, child, first : first + rows, :].astype(jnp.float32)
             avg_ref[slot, first : first + rows, :] = (total * factor).astype(jnp.bfloat16)
 
-    def body(k, _):
-        load(sent_slot(k)).wait()
-        averaged(sent_slot(k))
-        send_out(k).start()
-        load(other_slot(k)).wait()
-        averaged(other_slot(k))
+    def body(k, _, first):
+        load(first + k).wait()
+        averaged(first + k)
+        if first is first_sent:
+            send_out(k).start()
         return 0
 
-    def cross(first, many):
-        value = avg_ref[first : first + many].reshape(many * cells, width)
+    def cross(slot, many):
+        value = avg_ref[pl.ds(slot, many)].reshape(many * cells, width)
         return lax.dot_general(value, value, (((0,), (0,)), ((), ())), preferred_element_type=jnp.float32)
 
-    done = 0
-    for many in groups:
-        lax.fori_loop(done, done + many, body, 0)
-        part = cross(done, many) + cross(done + half, many)
-        acc[...] = part if done == 0 else acc[...] + part
-        done += many
+    acc[...] = jnp.zeros_like(acc)
+    for first, runs in zip((first_sent, first_kept), groups):
+        done = 0
+        for many in runs:
+            lax.fori_loop(done, done + many, functools.partial(body, first=first), 0)
+            acc[...] += cross(first + done, many)
+            done += many
     lane = lax.broadcasted_iota(jnp.int32, (width // 4, width), 1)
     strips = [acc[i : i + width // 4, :] * scale for i in range(0, width, width // 4)]
     second = jnp.where(lane < width // 4, pltpu.roll(strips[3], width // 4, 1), strips[1])
     cut = width // 8
     third = jnp.where(lane[:cut] < width // 2, pltpu.roll(strips[2][cut:], width // 2, 1), strips[2][:cut])
     packed = jnp.concatenate([strips[0], second, third], axis=0)
-    middle = packed.shape[0] // 2
-    top, low = packed[:middle], packed[middle:]
-    keep_ref[...] = jnp.where(parity == 0, top, low)
-    send_ref[...] = jnp.where(parity == 0, low, top)
+    members, cores, middle, _ = part_ref.shape
+    for core in range(cores):
+        for member in range(members):
+            part_ref[member, core] = packed[core * middle : (core + 1) * middle]
 
     def finish(k, _):
         send_out(k).wait()
@@ -186,6 +183,7 @@
         part = rest.astype(jnp.bfloat16)
         parts.append(part)
         rest = rest - part.astype(jnp.float32)
+    terms = jnp.concatenate(parts, axis=1)
 
     def store(i):
         return pltpu.make_async_copy(out.at[i], modes_ref.at[pl.ds(i * cells, cells)], out_sems.at[i])
@@ -197,26 +195,20 @@
         from_odd = jnp.where(wanted < excess, slots + wanted, wanted - excess)
         index = jnp.where(parity == 0, from_even, from_odd)
         value = buf[index]
-        total = jnp.zeros((cells, width), jnp.float32)
-        for part in reversed(parts):
-            total += lax.dot_general(value, part, (((1,), (1,)), ((), ())), preferred_element_type=jnp.float32)
+        repeated = jnp.concatenate([value] * len(parts), axis=1)
+        total = lax.dot_general(repeated, terms, (((1,), (1,)), ((), ())), preferred_element_type=jnp.float32)
         out[i] = total.astype(jnp.bfloat16)
         store(i).start()
     for i in range(blocks):
         store(i).wait()
 
 
-def spread_sum(value, axes, members):
-    sent = jnp.broadcast_to(value[None], (members,) + value.shape)
-    return jnp.sum(lax.all_to_all(sent, axes, 0, 0), axis=0)
-
-
 def swapped(value):
     return lax.ppermute(value, "c", [(0, 1), (1, 0)])
 
 
 def groups_of(total):
-    return [total // 4] * 3 + [total // 4 - 1, 1]
+    return [total], [total // 2, total // 2 - 2, 2]
 
 
 def shards(fine, patch_count, block_place):
@@ -228,16 +220,15 @@
     row_total = blocks * cells * devices
     vmem, hbm = pltpu.VMEM, pl.ANY
     spec = lambda space: pl.BlockSpec(memory_space=space)
-    own, outgoing, keep, send = pl.pallas_call(
+    own, outgoing, parts = pl.pallas_call(
         functools.partial(front_kernel, 1.0 / row_total, groups_of(blocks)),
         out_shape=(
             jax.ShapeDtypeStruct((slots, cells, width), jnp.bfloat16),
             jax.ShapeDtypeStruct((blocks, cells, width), jnp.bfloat16),
-            jax.ShapeDtypeStruct((width * 5 // 16, width), jnp.float32),
-            jax.ShapeDtypeStruct((width * 5 // 16, width), jnp.float32),
+            jax.ShapeDtypeStruct((lax.axis_size("z"), 2, width * 5 // 16, width), jnp.float32),
         ),
         in_specs=[spec(hbm), spec(hbm)],
-        out_specs=[spec(vmem), spec(hbm), spec(vmem), spec(vmem)],
+        out_specs=[spec(vmem), spec(pltpu.HBM), spec(vmem)],
         scratch_shapes=[
             pltpu.VMEM(fine.shape, jnp.bfloat16),
             pltpu.VMEM((width, width), jnp.float32),
@@ -249,11 +240,12 @@
         compiler_params=pltpu.CompilerParams(vmem_limit_bytes=50 * 2**20),
         name="front",
     )(patch_count, fine)
-    half = keep + swapped(send)
-    half, outgoing = lax.optimization_barrier((half, outgoing))
+    parts = parts.reshape((-1,) + parts.shape[2:])
+    half = jnp.sum(lax.all_to_all(parts, ("z", "c"), 0, 0), axis=0)
+
     moved = swapped(outgoing)
-    half = spread_sum(half, ("x", "y"), lax.axis_size("x") * lax.axis_size("y"))
-    half = spread_sum(half, ("z",), lax.axis_size("z"))
+    sent = jnp.broadcast_to(half[None], (lax.axis_size("x") * lax.axis_size("y"),) + half.shape)
+    half = jnp.sum(lax.all_to_all(sent, ("x", "y"), 0, 0), axis=0)
     other = swapped(half)
     factor, modes = pl.pallas_call(
         back_kernel,

time: 46.8 us -> 45.4 us (0.970)
  starting transfers between devices: 5.27 us -> 3.86 us
  blocking collectives: 24.2 us -> 25.2 us
  waiting for transfers between devices: 1.69 us -> 0.85 us
    ppermute x3 -> x2, starting transfers between devices: 5.27 us -> 3.86 us  [swapped(): return lax.ppermute(value, 'c', [(0, 1), (1, 0)])]
    all_to_all x2, blocking collectives: 24.2 us -> 25.2 us  [the longest x1 14.4 us: shards(): half = jnp.sum(lax.all_to_all(sent, ('x', 'y'), 0, 0), axis=0)]
    ppermute x3 -> x2, waiting for transfers between devices: 1.69 us -> 0.85 us  [swapped(): return lax.ppermute(value, 'c', [(0, 1), (1, 0)])]
  transfers between devices with their start and end apart: 3 -> 2, of which waited for: 2 -> 1; matrix products, arithmetic and copies ran while one was open for 0% -> 0% of each run, Pallas kernels for 0% -> 0%
where the time goes in v3:
time: 45.4 us; the launch traced here: 45.2 us
  blocking collectives  25.2 us (56%)
  Pallas kernels  13.9 us (31%)
  starting transfers between devices  3.86 us (9%)
  between operations  1.32 us (3%)
  waiting for transfers between devices  0.85 us (2%)
    all_to_all x1, blocking collectives, shards(): half = jnp.sum(lax.all_to_all(sent, ('x', 'y'), 0, 0), axis=0)  14.4 us
    all_to_all x1, blocking collectives, shards(): half = jnp.sum(lax.all_to_all(parts, ('z', 'c'), 0, 0), axis=0)  10.9 us
    pallas_call x1, Pallas kernels, shards(): pl.pallas_call(functools.partial(front_kernel, 1.0 / row_total, groups_of...  7.26 us
    pallas_call x1, Pallas kernels, shards(): pl.pallas_call(back_kernel, out_shape=(jax.ShapeDtypeStruct((width, width...  6.67 us
    ppermute x2, starting transfers between devices, swapped(): return lax.ppermute(value, 'c', [(0, 1), (1, 0)])  3.86 us
  transfers between devices with their start and end apart: 2, of which 1 were waited for; matrix products, arithmetic and copies ran while one was open for 0% of the time, Pallas kernels for 0%

profile of v3, /device:TPU:1, one launch (start us, length us, event | category | flops | bytes accessed | tf_op | source)
XLA Modules:
  0.0 45.2 jit_solution(11161318414296600288)
XLA Ops:
  0.6 0.0 copy-start
  1.3 7.3 %front.1 = (bf16[32,256,128]{2,1,0:T(8,128)(2,1)S(1)}, bf16[16,256,128]{2,1,0:T(8,128)(2,1)}, f32[4,2,40,128]{3,2,1,0:T(8,128)S(1)}) custom-call(s32[1]{0:T(128)S(6)} %copy.5.count_hbm, bf16[32,8,256,128]{3,2,1,0:T(8,128)(2,1)} %fine_ref.1), custom_call_target="tpu_custom_call" | custom-call | tf_op jit(solution)/shard_map/front/pallas_call | solution.py:223
  8.6 1.5 %collective-permute-start.1 = (bf16[16,256,128]{2,1,0:T(8,128)(2,1)}, bf16[16,256,128]{2,1,0:T(8,128)(2,1)S(1)}, u32[]{:S(2)}, u32[]{:S(2)}) collective-permute-start(bf16[16,256,128]{2,1,0:T(8,128)(2,1)} %get-tuple-element.7), channel_id=1, source_target_pairs={{0,1},{1,0},{2,3},{3,2},{4,5},{5,4},{6,7},{7,6},{8,9},{9,8},{10,11... | collective-permute-start | bytes 3145736 | tf_op jit(solution)/shard_map/ppermute | solution.py:207
  10.0 10.9 %all_to_all.10 = f32[8,40,128]{2,1,0:T(8,128)S(1)} all-to-all(f32[8,40,128]{2,1,0:T(8,128)S(1)} %bitcast.1), channel_id=1, replica_groups=mesh['x'=4,'y'=4,'z'=4,'c'=2] {'z','c'}, dimensions={0} | all-to-all | bytes 327680 | tf_op jit(solution)/shard_map/all_to_all | solution.py:244
  20.9 14.4 %all_to_all.11 = f32[16,40,128]{2,1,0:T(8,128)S(1)} all-to-all(f32[16,40,128]{2,1,0:T(8,128)S(1)} %broadcast_in_dim.2), channel_id=1, replica_groups=mesh['x'=4,'y'=4,'z'=4,'c'=2] {'x','y'}, dimensions={0} | all-to-all | bytes 655360 | tf_op jit(solution)/shard_map/all_to_all | solution.py:248
  35.3 2.4 %collective-permute-start = (f32[40,128]{1,0:T(8,128)S(1)}, f32[40,128]{1,0:T(8,128)S(1)}, u32[]{:S(2)}, u32[]{:S(2)}) collective-permute-start(f32[40,128]{1,0:T(8,128)S(1)} %reduce_sum.19.mine_ref), channel_id=1, source_target_pairs={{0,1},{1,0},{2,3},{3,2},{4,5},{5,4},{6,7},{7,6},{8,9},{9,8},{10,11... | collective-permute-start | bytes 61448 | tf_op jit(solution)/shard_map/ppermute | solution.py:207
  37.7 0.8 %collective-permute-done.other_ref = f32[40,128]{1,0:T(8,128)S(1)} collective-permute-done((f32[40,128]{1,0:T(8,128)S(1)}, f32[40,128]{1,0:T(8,128)S(1)}, u32[]{:S(2)}, u32[]{:S(2)}) %collective-permute-start) | collective-permute-done | bytes 20512 | tf_op jit(solution)/shard_map/ppermute | solution.py:207
  38.6 0.0 collective-permute-done.1.moved_ref
  38.6 0.0 copy-done
  38.6 6.7 %back.1 = (f32[128,128]{1,0:T(8,128)}, bf16[4096,128]{1,0:T(8,128)(2,1)}) custom-call(s32[1]{0:T(128)S(6)} %copy.5.count_hbm, s32[1,16]{1,0:T(1,128)S(1)} %copy-done, f32[40,128]{1,0:T(8,128)S(1)} %reduce_sum.19.mine_ref, f32[40,128]{1,0:T(8,128)S(1)} %collective-permute-done.other_ref, bf16[32,256,128]{2,1,0:T(8,128)(2,1)S(1)} %get-tuple-element.6.own_ref, ...), custom_call_target="tpu_custom_call" | custom-call | tf_op jit(solution)/shard_map/back/pallas_call | solution.py:250
  (3 shorter events, 0.1 us)
Async XLA Ops:
  0.6 37.9 %copy-start = (s32[1,16]{1,0:T(1,128)S(1)}, s32[1,16]{1,0:T(1,128)}, u32[]{:S(2)}) copy-start(s32[1,16]{1,0:T(1,128)} %place_hbm.1) | copy-start | bytes 196
  8.6 30.0 %collective-permute-start.1 = (bf16[16,256,128]{2,1,0:T(8,128)(2,1)}, bf16[16,256,128]{2,1,0:T(8,128)(2,1)S(1)}, u32[]{:S(2)}, u32[]{:S(2)}) collective-permute-start(bf16[16,256,128]{2,1,0:T(8,128)(2,1)} %get-tuple-element.7), channel_id=1, source_target_pairs={{0,1},{1,0},{2,3},{3,2},{4,5},{5,4},{6,7},{7,6},{8,9},{9,8},{10,11... | collective-permute-start | bytes 3145736 | tf_op jit(solution)/shard_map/ppermute | solution.py:207
  35.3 3.2 %collective-permute-start = (f32[40,128]{1,0:T(8,128)S(1)}, f32[40,128]{1,0:T(8,128)S(1)}, u32[]{:S(2)}, u32[]{:S(2)}) collective-permute-start(f32[40,128]{1,0:T(8,128)S(1)} %reduce_sum.19.mine_ref), channel_id=1, source_target_pairs={{0,1},{1,0},{2,3},{3,2},{4,5},{5,4},{6,7},{7,6},{8,9},{9,8},{10,11... | collective-permute-start | bytes 61448 | tf_op jit(solution)/shard_map/ppermute | solution.py:207

commit v4 on v3

--- a/solution.py
+++ b/solution.py
@@ -109,47 +109,80 @@
     return jnp.broadcast_to(tile[row : row + 1, :], tile.shape)
 
 
-def eliminate(rows):
+def three_terms(value):
+    terms = []
+    for _ in range(3):
+        term = value.astype(jnp.bfloat16)
+        terms.append(term)
+        value = value - term.astype(jnp.float32)
+    return terms
+
+
+def eliminate(rows, near=3):
     shape = rows[0].shape
     lane = lax.broadcasted_iota(jnp.int32, shape, 1)
     sub = lax.broadcasted_iota(jnp.int32, shape, 0)
+    zero = lane.astype(jnp.float32) * 0.0
     rows = list(rows)
+    tiles = len(rows)
     factor, inverse = [], []
-    for t in range(len(rows)):
+
+    def columns_of(tile, base):
+        return [lane_spread(tile, base + c) + zero for c in range(TILE)]
+
+    ahead = columns_of(rows[0], 0)
+    for t in range(tiles):
         base = t * TILE
         inside = (lane >= base) & (lane < base + TILE)
-        panel = rows[t]
-        columns = [lane_spread(panel, base + c) for c in range(TILE)]
-        d = [[row_spread(columns[c], i) for c in range(i + 1)] for i in range(TILE)]
-        upper = [row_spread(panel, i) for i in range(TILE)]
-        mixed = [jnp.where(inside, (lane == base + i).astype(jnp.float32), upper[i]) for i in range(TILE)]
+        last = min(tiles, t + 1 + near)
+        columns = {j: columns_of(rows[j], base) for j in range(t + 1, last)}
+        after = columns_of(rows[t + 1], base + TILE) if t + 1 < tiles else None
+        d = [[row_spread(ahead[c], i) for c in range(i + 1)] for i in range(TILE)]
+        mixed = [
+            jnp.where(inside, (lane == base + i).astype(jnp.float32), row_spread(rows[t], i)) for i in range(TILE)
+        ]
         inv = [None] * TILE
         for r in range(TILE):
             inv[r] = lax.rsqrt(d[r][r])
             for i in range(r + 1, TILE):
                 d[i][r] = d[i][r] * inv[r]
             mixed[r] = mixed[r] * inv[r]
-            upper[r] = upper[r] * inv[r]
             for i in range(r + 1, TILE):
                 for c in range(r + 1, i + 1):
                     d[i][c] = d[i][c] - d[i][r] * d[c][r]
                 mixed[i] = mixed[i] - d[i][r] * mixed[r]
-                upper[i] = upper[i] - d[i][r] * upper[r]
-        for j in range(t + 1, len(rows)):
-            b = [lane_spread(rows[j], base + c) for c in range(TILE)]
-            z = jnp.where(inside, 0.0, rows[j])
+        for j in range(t + 1, last):
+            b = columns[j]
+            rest = jnp.where(inside, 0.0, rows[j])
             for r in range(TILE):
                 b[r] = b[r] * inv[r]
                 for c in range(r + 1, TILE):
                     b[c] = b[c] - b[r] * d[c][r]
-                z = z - b[r] * mixed[r]
-            rows[j] = z
-        f, m = jnp.zeros(shape, jnp.float32), jnp.zeros(shape, jnp.float32)
-        for r in range(TILE):
-            f = jnp.where((sub == r) & (lane >= base + r), upper[r], f)
-            m = jnp.where((sub == r) & (lane <= base + r), mixed[r], m)
-        factor.append(f)
-        inverse.append(m)
+                rest = rest - b[r] * mixed[r]
+                if j == t + 1:
+                    for c in range(TILE):
+                        after[c] = after[c] - b[r] * row_spread(b[r], c)
+            rows[j] = rest
+        ahead = after
+        whole = mixed[0]
+        for r in range(1, TILE):
+            whole = jnp.where(sub == r, mixed[r], whole)
+        past = lane >= base + TILE
+        upper = jnp.where(past, whole, 0.0)
+        if last < tiles:
+            u, y = three_terms(upper), three_terms(whole)
+            left = jnp.concatenate([u[0], u[0], u[1], u[1], u[0], u[2]], axis=0)
+            right = jnp.concatenate([y[0], y[1], y[0], y[1], y[2], y[0]], axis=0)
+            product = lax.dot_general(left, right, (((0,), (0,)), ((), ())), preferred_element_type=jnp.float32)
+            for j in range(last, tiles):
+                rows[j] = jnp.where(inside, 0.0, rows[j]) - product[j * TILE : (j + 1) * TILE]
+        for c in range(TILE):
+            column = d[c][c] * inv[c]
+            for r in range(c):
+                column = jnp.where(sub == r, d[c][r], column)
+            upper = jnp.where((lane == base + c) & (sub <= c), column, upper)
+        factor.append(upper)
+        inverse.append(jnp.where(past, 0.0, whole))
     return factor, inverse
 
 
@@ -177,13 +210,10 @@
     for load in loads:
         load.wait()
     count = count_ref[0]
-    rest = inv[...]
-    parts = []
-    for _ in range(3):
-        part = rest.astype(jnp.bfloat16)
-        parts.append(part)
-        rest = rest - part.astype(jnp.float32)
-    terms = jnp.concatenate(parts, axis=1)
+    parts = three_terms(inv[...])
+    terms = jnp.concatenate(
+        [jnp.concatenate(parts[:2], axis=1), jnp.concatenate([parts[2], jnp.zeros_like(parts[2])], axis=1)], axis=0
+    )
 
     def store(i):
         return pltpu.make_async_copy(out.at[i], modes_ref.at[pl.ds(i * cells, cells)], out_sems.at[i])
@@ -195,8 +225,9 @@
         from_odd = jnp.where(wanted < excess, slots + wanted, wanted - excess)
         index = jnp.where(parity == 0, from_even, from_odd)
         value = buf[index]
-        repeated = jnp.concatenate([value] * len(parts), axis=1)
-        total = lax.dot_general(repeated, terms, (((1,), (1,)), ((), ())), preferred_element_type=jnp.float32)
+        repeated = jnp.concatenate([value, value], axis=1)
+        both = lax.dot_general(repeated, terms, (((1,), (1,)), ((), ())), preferred_element_type=jnp.float32)
+        total = both[:, :width] + both[:, width:]
         out[i] = total.astype(jnp.bfloat16)
         store(i).start()
     for i in range(blocks):

time: 45.4 us -> 43.9 us (0.967)
  Pallas kernels: 13.9 us -> 12.3 us
    pallas_call x1, Pallas kernels: 6.67 us -> 5.08 us  [shards(): pl.pallas_call(back_kernel, out_shape=(jax.ShapeDtypeStruct((width, width...]
where the time goes in v4:
time: 43.9 us; the launch traced here: 43.7 us
  blocking collectives  25.2 us (57%)
  Pallas kernels  12.3 us (28%)
  starting transfers between devices  3.86 us (9%)
  between operations  1.32 us (3%)
  waiting for transfers between devices  0.85 us (2%)
    all_to_all x1, blocking collectives, shards(): half = jnp.sum(lax.all_to_all(sent, ('x', 'y'), 0, 0), axis=0)  14.4 us
    all_to_all x1, blocking collectives, shards(): half = jnp.sum(lax.all_to_all(parts, ('z', 'c'), 0, 0), axis=0)  10.9 us
    pallas_call x1, Pallas kernels, shards(): pl.pallas_call(functools.partial(front_kernel, 1.0 / row_total, groups_of...  7.26 us
    pallas_call x1, Pallas kernels, shards(): pl.pallas_call(back_kernel, out_shape=(jax.ShapeDtypeStruct((width, width...  5.08 us
    ppermute x2, starting transfers between devices, swapped(): return lax.ppermute(value, 'c', [(0, 1), (1, 0)])  3.86 us
  transfers between devices with their start and end apart: 2, of which 1 were waited for; matrix products, arithmetic and copies ran while one was open for 0% of the time, Pallas kernels for 0%

profile of v4, /device:TPU:1, one launch (start us, length us, event | category | flops | bytes accessed | tf_op | source)
XLA Modules:
  0.0 43.7 jit_solution(3929325743496106867)
XLA Ops:
  0.6 0.0 copy-start
  1.3 7.3 %front.1 = (bf16[32,256,128]{2,1,0:T(8,128)(2,1)S(1)}, bf16[16,256,128]{2,1,0:T(8,128)(2,1)}, f32[4,2,40,128]{3,2,1,0:T(8,128)S(1)}) custom-call(s32[1]{0:T(128)S(6)} %copy.5.count_hbm, bf16[32,8,256,128]{3,2,1,0:T(8,128)(2,1)} %fine_ref.1), custom_call_target="tpu_custom_call" | custom-call | tf_op jit(solution)/shard_map/front/pallas_call | solution.py:254
  8.6 1.5 %collective-permute-start.1 = (bf16[16,256,128]{2,1,0:T(8,128)(2,1)}, bf16[16,256,128]{2,1,0:T(8,128)(2,1)S(1)}, u32[]{:S(2)}, u32[]{:S(2)}) collective-permute-start(bf16[16,256,128]{2,1,0:T(8,128)(2,1)} %get-tuple-element.7), channel_id=1, source_target_pairs={{0,1},{1,0},{2,3},{3,2},{4,5},{5,4},{6,7},{7,6},{8,9},{9,8},{10,11... | collective-permute-start | bytes 3145736 | tf_op jit(solution)/shard_map/ppermute | solution.py:238
  10.0 10.9 %all_to_all.10 = f32[8,40,128]{2,1,0:T(8,128)S(1)} all-to-all(f32[8,40,128]{2,1,0:T(8,128)S(1)} %bitcast.1), channel_id=1, replica_groups=mesh['x'=4,'y'=4,'z'=4,'c'=2] {'z','c'}, dimensions={0} | all-to-all | bytes 327680 | tf_op jit(solution)/shard_map/all_to_all | solution.py:275
  20.9 14.4 %all_to_all.11 = f32[16,40,128]{2,1,0:T(8,128)S(1)} all-to-all(f32[16,40,128]{2,1,0:T(8,128)S(1)} %broadcast_in_dim.2), channel_id=1, replica_groups=mesh['x'=4,'y'=4,'z'=4,'c'=2] {'x','y'}, dimensions={0} | all-to-all | bytes 655360 | tf_op jit(solution)/shard_map/all_to_all | solution.py:279
  35.3 2.4 %collective-permute-start = (f32[40,128]{1,0:T(8,128)S(1)}, f32[40,128]{1,0:T(8,128)S(1)}, u32[]{:S(2)}, u32[]{:S(2)}) collective-permute-start(f32[40,128]{1,0:T(8,128)S(1)} %reduce_sum.19.mine_ref), channel_id=1, source_target_pairs={{0,1},{1,0},{2,3},{3,2},{4,5},{5,4},{6,7},{7,6},{8,9},{9,8},{10,11... | collective-permute-start | bytes 61448 | tf_op jit(solution)/shard_map/ppermute | solution.py:238
  37.7 0.8 %collective-permute-done.other_ref = f32[40,128]{1,0:T(8,128)S(1)} collective-permute-done((f32[40,128]{1,0:T(8,128)S(1)}, f32[40,128]{1,0:T(8,128)S(1)}, u32[]{:S(2)}, u32[]{:S(2)}) %collective-permute-start) | collective-permute-done | bytes 20512 | tf_op jit(solution)/shard_map/ppermute | solution.py:238
  38.6 0.0 collective-permute-done.1.moved_ref
  38.6 0.0 copy-done
  38.6 5.1 %back.1 = (f32[128,128]{1,0:T(8,128)}, bf16[4096,128]{1,0:T(8,128)(2,1)}) custom-call(s32[1]{0:T(128)S(6)} %copy.5.count_hbm, s32[1,16]{1,0:T(1,128)S(1)} %copy-done, f32[40,128]{1,0:T(8,128)S(1)} %reduce_sum.19.mine_ref, f32[40,128]{1,0:T(8,128)S(1)} %collective-permute-done.other_ref, bf16[32,256,128]{2,1,0:T(8,128)(2,1)S(1)} %get-tuple-element.6.own_ref, ...), custom_call_target="tpu_custom_call" | custom-call | tf_op jit(solution)/shard_map/back/pallas_call | solution.py:281
  (3 shorter events, 0.1 us)
Async XLA Ops:
  0.6 37.9 %copy-start = (s32[1,16]{1,0:T(1,128)S(1)}, s32[1,16]{1,0:T(1,128)}, u32[]{:S(2)}) copy-start(s32[1,16]{1,0:T(1,128)} %place_hbm.1) | copy-start | bytes 196
  8.6 30.0 %collective-permute-start.1 = (bf16[16,256,128]{2,1,0:T(8,128)(2,1)}, bf16[16,256,128]{2,1,0:T(8,128)(2,1)S(1)}, u32[]{:S(2)}, u32[]{:S(2)}) collective-permute-start(bf16[16,256,128]{2,1,0:T(8,128)(2,1)} %get-tuple-element.7), channel_id=1, source_target_pairs={{0,1},{1,0},{2,3},{3,2},{4,5},{5,4},{6,7},{7,6},{8,9},{9,8},{10,11... | collective-permute-start | bytes 3145736 | tf_op jit(solution)/shard_map/ppermute | solution.py:238
  35.3 3.2 %collective-permute-start = (f32[40,128]{1,0:T(8,128)S(1)}, f32[40,128]{1,0:T(8,128)S(1)}, u32[]{:S(2)}, u32[]{:S(2)}) collective-permute-start(f32[40,128]{1,0:T(8,128)S(1)} %reduce_sum.19.mine_ref), channel_id=1, source_target_pairs={{0,1},{1,0},{2,3},{3,2},{4,5},{5,4},{6,7},{7,6},{8,9},{9,8},{10,11... | collective-permute-start | bytes 61448 | tf_op jit(solution)/shard_map/ppermute | solution.py:238

commit v5 on v4

--- a/solution.py
+++ b/solution.py
@@ -128,9 +128,9 @@
     factor, inverse = [], []
 
     def columns_of(tile, base):
-        return [lane_spread(tile, base + c) + zero for c in range(TILE)]
-
-    ahead = columns_of(rows[0], 0)
+        return [lane_spread(tile, base + c) for c in range(TILE)]
+
+    ahead = [column + zero for column in columns_of(rows[0], 0)]
     for t in range(tiles):
         base = t * TILE
         inside = (lane >= base) & (lane < base + TILE)

time: 43.9 us -> 43.8 us (level)
  no operation moved by 1% of the time
where the time goes in v5:
time: 43.8 us; the launch traced here: 43.6 us
  blocking collectives  25.2 us (58%)
  Pallas kernels  12.3 us (28%)
  starting transfers between devices  3.86 us (9%)
  between operations  1.32 us (3%)
  waiting for transfers between devices  0.85 us (2%)
    all_to_all x1, blocking collectives, shards(): half = jnp.sum(lax.all_to_all(sent, ('x', 'y'), 0, 0), axis=0)  14.4 us
    all_to_all x1, blocking collectives, shards(): half = jnp.sum(lax.all_to_all(parts, ('z', 'c'), 0, 0), axis=0)  10.9 us
    pallas_call x1, Pallas kernels, shards(): pl.pallas_call(functools.partial(front_kernel, 1.0 / row_total, groups_of...  7.26 us
    pallas_call x1, Pallas kernels, shards(): pl.pallas_call(back_kernel, out_shape=(jax.ShapeDtypeStruct((width, width...  5.06 us
    ppermute x2, starting transfers between devices, swapped(): return lax.ppermute(value, 'c', [(0, 1), (1, 0)])  3.86 us
  transfers between devices with their start and end apart: 2, of which 1 were waited for; matrix products, arithmetic and copies ran while one was open for 0% of the time, Pallas kernels for 0%

profile of v5, /device:TPU:1, one launch (start us, length us, event | category | flops | bytes accessed | tf_op | source)
XLA Modules:
  0.0 43.6 jit_solution(10830531067742808536)
XLA Ops:
  0.6 0.0 copy-start
  1.3 7.3 %front.1 = (bf16[32,256,128]{2,1,0:T(8,128)(2,1)S(1)}, bf16[16,256,128]{2,1,0:T(8,128)(2,1)}, f32[4,2,40,128]{3,2,1,0:T(8,128)S(1)}) custom-call(s32[1]{0:T(128)S(6)} %copy.5.count_hbm, bf16[32,8,256,128]{3,2,1,0:T(8,128)(2,1)} %fine_ref.1), custom_call_target="tpu_custom_call" | custom-call | tf_op jit(solution)/shard_map/front/pallas_call | solution.py:254
  8.6 1.5 %collective-permute-start.1 = (bf16[16,256,128]{2,1,0:T(8,128)(2,1)}, bf16[16,256,128]{2,1,0:T(8,128)(2,1)S(1)}, u32[]{:S(2)}, u32[]{:S(2)}) collective-permute-start(bf16[16,256,128]{2,1,0:T(8,128)(2,1)} %get-tuple-element.7), channel_id=1, source_target_pairs={{0,1},{1,0},{2,3},{3,2},{4,5},{5,4},{6,7},{7,6},{8,9},{9,8},{10,11... | collective-permute-start | bytes 3145736 | tf_op jit(solution)/shard_map/ppermute | solution.py:238
  10.0 10.9 %all_to_all.10 = f32[8,40,128]{2,1,0:T(8,128)S(1)} all-to-all(f32[8,40,128]{2,1,0:T(8,128)S(1)} %bitcast.1), channel_id=1, replica_groups=mesh['x'=4,'y'=4,'z'=4,'c'=2] {'z','c'}, dimensions={0} | all-to-all | bytes 327680 | tf_op jit(solution)/shard_map/all_to_all | solution.py:275
  20.9 14.4 %all_to_all.11 = f32[16,40,128]{2,1,0:T(8,128)S(1)} all-to-all(f32[16,40,128]{2,1,0:T(8,128)S(1)} %broadcast_in_dim.2), channel_id=1, replica_groups=mesh['x'=4,'y'=4,'z'=4,'c'=2] {'x','y'}, dimensions={0} | all-to-all | bytes 655360 | tf_op jit(solution)/shard_map/all_to_all | solution.py:279
  35.3 2.4 %collective-permute-start = (f32[40,128]{1,0:T(8,128)S(1)}, f32[40,128]{1,0:T(8,128)S(1)}, u32[]{:S(2)}, u32[]{:S(2)}) collective-permute-start(f32[40,128]{1,0:T(8,128)S(1)} %reduce_sum.19.mine_ref), channel_id=1, source_target_pairs={{0,1},{1,0},{2,3},{3,2},{4,5},{5,4},{6,7},{7,6},{8,9},{9,8},{10,11... | collective-permute-start | bytes 61448 | tf_op jit(solution)/shard_map/ppermute | solution.py:238
  37.7 0.8 %collective-permute-done.other_ref = f32[40,128]{1,0:T(8,128)S(1)} collective-permute-done((f32[40,128]{1,0:T(8,128)S(1)}, f32[40,128]{1,0:T(8,128)S(1)}, u32[]{:S(2)}, u32[]{:S(2)}) %collective-permute-start) | collective-permute-done | bytes 20512 | tf_op jit(solution)/shard_map/ppermute | solution.py:238
  38.6 0.0 collective-permute-done.1.moved_ref
  38.6 0.0 copy-done
  38.6 5.1 %back.1 = (f32[128,128]{1,0:T(8,128)}, bf16[4096,128]{1,0:T(8,128)(2,1)}) custom-call(s32[1]{0:T(128)S(6)} %copy.5.count_hbm, s32[1,16]{1,0:T(1,128)S(1)} %copy-done, f32[40,128]{1,0:T(8,128)S(1)} %reduce_sum.19.mine_ref, f32[40,128]{1,0:T(8,128)S(1)} %collective-permute-done.other_ref, bf16[32,256,128]{2,1,0:T(8,128)(2,1)S(1)} %get-tuple-element.6.own_ref, ...), custom_call_target="tpu_custom_call" | custom-call | tf_op jit(solution)/shard_map/back/pallas_call | solution.py:281
  (3 shorter events, 0.1 us)
Async XLA Ops:
  0.6 37.9 %copy-start = (s32[1,16]{1,0:T(1,128)S(1)}, s32[1,16]{1,0:T(1,128)}, u32[]{:S(2)}) copy-start(s32[1,16]{1,0:T(1,128)} %place_hbm.1) | copy-start | bytes 196
  8.6 30.0 %collective-permute-start.1 = (bf16[16,256,128]{2,1,0:T(8,128)(2,1)}, bf16[16,256,128]{2,1,0:T(8,128)(2,1)S(1)}, u32[]{:S(2)}, u32[]{:S(2)}) collective-permute-start(bf16[16,256,128]{2,1,0:T(8,128)(2,1)} %get-tuple-element.7), channel_id=1, source_target_pairs={{0,1},{1,0},{2,3},{3,2},{4,5},{5,4},{6,7},{7,6},{8,9},{9,8},{10,11... | collective-permute-start | bytes 3145736 | tf_op jit(solution)/shard_map/ppermute | solution.py:238
  35.3 3.2 %collective-permute-start = (f32[40,128]{1,0:T(8,128)S(1)}, f32[40,128]{1,0:T(8,128)S(1)}, u32[]{:S(2)}, u32[]{:S(2)}) collective-permute-start(f32[40,128]{1,0:T(8,128)S(1)} %reduce_sum.19.mine_ref), channel_id=1, source_target_pairs={{0,1},{1,0},{2,3},{3,2},{4,5},{5,4},{6,7},{7,6},{8,9},{9,8},{10,11... | collective-permute-start | bytes 61448 | tf_op jit(solution)/shard_map/ppermute | solution.py:238
